TPU v7x, 256 devices: a whole 4x4x8 slice. The times are simulated.
256 devices in a mesh: region: 32 (over x, z), comm: 8 (over y, core).
Axes of the slice: x: 4, y: 4, z: 8, core: 2. Of those that a mesh axis runs over, the one named last changes fastest.
Arguments:
- cost: float32 [128, 262144], P('comm', 'region'), may hold values from 0.01 to 15, as said below
- flow_start: float32 [128, 262144], P('comm', 'region'), may hold values from 0 to 0.5
- capacity: float32 [262144], P('region'), may hold values from 5 to 135, as said below
- cap_dual_start: float32 [262144], P('region'), may hold values from 0 to 1
- demand: float32 [128, 131072], P('comm', 'region'), may hold values from -24 to 24
- node_dual_start: float32 [128, 131072], P('comm', 'region'), may hold values from -6 to 6
- incidence: float32 [4096, 128, 128], P('region'), may hold values from -0.25 to 0.25
- block_node: int32 [4096], P('region'), may hold values from 0 to 39
- ghost_source: int32 [256], P('region'), may hold values from 0 to 127, as said below
Outputs:
- final_flow: float32 [128, 262144], P('comm', 'region')
- final_cap_dual: float32 [262144], P('region')
- final_node_dual: float32 [128, 131072], P('comm', 'region')
Inputs may be any that keep to these rules, and one draw needn't show every extreme that they name: Each cost is positive. Each capacity is positive. `ghost_source`: ghost slot g of region r names boundary block j of region q as q * 4 + j. Slot 0 of every region has q = r + 16 in cyclic order; every other slot has q at most two regions from r in cyclic order (q may be r).
All inputs are finite; a program needn't handle non-finite values.
Results may differ from a plain program's by a relative error of at most 0.00021.
Values sent between devices are 32-bit elements; how exact they have to be, the bound alone decides.
A program may use at most 64 MiB of HBM per device.

v0:
```python
import jax
import jax.numpy as jnp
from jax import lax
from jax.sharding import PartitionSpec as P

BPA = 2
NBD = 4
NG = 8
ITERS = 2
step_scale = 0.08
highest = lax.Precision.HIGHEST


def pick_blocks(bnd_table, indices, commodities, count, block_width):
    return jnp.take(bnd_table.reshape(commodities, count, block_width), indices, axis=1)


def body(
    cost,
    flow_start,
    capacity,
    cap_dual_start,
    demand,
    node_dual_start,
    incidence,
    block_node,
    ghost_source,
):
    commodities, arc_count = cost.shape
    block_count, block_width, _ = incidence.shape
    own_blocks = demand.shape[1] // block_width
    region_total = lax.axis_size("region")
    bound_all = region_total * NBD
    slot_count = own_blocks + NG
    cost_sq = jnp.sum(cost * cost)
    demand_sq = jnp.sum(demand * demand)
    capacity_sq = jnp.sum(capacity * capacity)
    cost_all, demand_all = lax.psum((cost_sq, demand_sq), ("region", "comm"))
    capacity_all = lax.psum(capacity_sq, "region")
    weight = jnp.sqrt(cost_all / (demand_all + capacity_all))
    primal_step = step_scale / weight
    dual_step = step_scale * weight
    slot_table = (block_node[:, None] == jnp.arange(slot_count, dtype=jnp.int32)[None, :]).astype(
        jnp.float32
    )
    ghost_table = (ghost_source[:, None] == jnp.arange(bound_all, dtype=jnp.int32)[None, :]).astype(
        jnp.float32
    )
    flow_now, cap_dual, node_dual = (flow_start, cap_dual_start, node_dual_start)
    edge_cols = NBD * block_width
    for iteration in range(ITERS):
        bnd_table = lax.all_gather(node_dual[:, :edge_cols], "region", axis=1, tiled=True)
        ghost_duals = pick_blocks(bnd_table, ghost_source, commodities, bound_all, block_width)
        dual_blocks = jnp.concatenate(
            [node_dual.reshape(commodities, own_blocks, block_width), ghost_duals], axis=1
        )
        chosen_duals = jnp.take(dual_blocks, block_node, axis=1)
        back_term = jnp.einsum("kbn,bna->kba", chosen_duals, incidence, precision=highest)
        back_term = (
            back_term.reshape(commodities, block_count // BPA, BPA, block_width)
            .sum(axis=2)
            .reshape(commodities, arc_count)
        )
        flow_new = jnp.maximum(flow_now - primal_step * (cost - back_term + cap_dual[None, :]), 0.0)
        flow_bar = 2.0 * flow_new - flow_now
        arc_load = jnp.sum(flow_bar, axis=0)
        load_total = lax.psum(arc_load, "comm")
        cap_dual = jnp.maximum(cap_dual + dual_step * (load_total - capacity), 0.0)
        repeated_flow = jnp.repeat(
            flow_bar.reshape(commodities, arc_count // block_width, block_width), BPA, axis=1
        )
        forward = jnp.einsum("kba,bna->kbn", repeated_flow, incidence, precision=highest)
        slot_rows = jnp.einsum("kbn,bs->ksn", forward, slot_table, precision=highest)
        own_rows = slot_rows[:, :own_blocks]
        routed = jnp.einsum(
            "kgn,gb->kbn", slot_rows[:, own_blocks:], ghost_table, precision=highest
        )
        arrived = lax.psum_scatter(routed, "region", scatter_dimension=1, tiled=True)
        node_rows = jnp.concatenate([own_rows[:, :NBD] + arrived, own_rows[:, NBD:]], axis=1)
        node_dual = node_dual + dual_step * (
            demand - node_rows.reshape(commodities, own_blocks * block_width)
        )
        flow_now = flow_new
    return (flow_now, cap_dual, node_dual)


def solution(mesh):
    return jax.shard_map(
        body,
        mesh=mesh,
        in_specs=(
            P("comm", "region"),
            P("comm", "region"),
            P("region"),
            P("region"),
            P("comm", "region"),
            P("comm", "region"),
            P("region", None, None),
            P("region"),
            P("region"),
        ),
        out_specs=(P("comm", "region"), P("region"), P("comm", "region")),
        check_vma=False,
    )
```

profile of v0, /device:TPU:8, one launch (start us, length us, event | category | flops | bytes accessed | tf_op | source)
XLA Modules:
  0.0 738.6 jit_solution(913210635620972559)
XLA Ops:
  7.2 1.5 slice.30
  8.8 1.6 multiply_reduce_fusion.1
  10.4 1.8 multiply_reduce_fusion
  12.2 1.4 multiply_reduce_fusion.2
  13.6 79.2 %all-reduce = (f32[]{:T(128)}, f32[]{:T(128)}) all-reduce(f32[]{:T(128)} %multiply_reduce_fusion, f32[]{:T(128)} %multiply_reduce_fusion.1), channel_id=1, replica_groups=mesh['region'=32,'comm'=8] {'region','comm'}, use_global_device_ids=true, to_apply=%region_1.0 | all-reduce | flops 2 | bytes 16 | tf_op jit(solution)/shard_map/psum | solution.py:38
  92.9 73.2 %psum.37 = f32[]{:T(128)} all-reduce(f32[]{:T(128)} %multiply_reduce_fusion.2), channel_id=1, replica_groups=mesh['region'=32,'comm'=8] {'region'}, use_global_device_ids=true, to_apply=%region_5.0 | all-reduce | flops 1 | bytes 8 | tf_op jit(solution)/shard_map/psum | solution.py:39
  168.2 0.7 compare_select_fusion.1
  169.5 0.7 compare_and_fusion
  170.1 0.7 compare_and_fusion.1
  170.8 1.0 copy_bitcast_fusion.5
  171.8 1.3 copy_bitcast_fusion.1
  173.8 0.8 gather_fusion.1
  174.6 9.6 %bitcast_reduce_fusion.1 = f32[16,64,128]{2,0,1:T(8,128)S(1)} fusion(f32[128,128,128]{2,1,0:T(8,128)} %param.19, f32[128,16,128]{2,1,0:T(8,128)S(1)} %gather_fusion.1, pred[128]{0:T(512)(128)(4,1)S(1)} %compare_and_fusion), kind=kOutput, calls=%fused_computation.13 | convolution fusion | flops 403046400 | bytes 9961600 | tf_op jit(solution)/shard_map/kbn,bna->kba/dot_general | solution.py:58
  184.7 15.4 %convolution_bitcast_fusion.1 = f32[16,128,128]{2,0,1:T(8,128)S(1)} fusion(f32[16,128,128]{2,0,1:T(8,128)S(1)} %bitcast.122, f32[128,128,128]{2,1,0:T(8,128)} %param.19), kind=kOutput, calls=%fused_computation.5 | convolution fusion | flops 402653184 | bytes 10485760 | tf_op jit(solution)/shard_map/kba,bna->kbn/dot_general | solution.py:72
  200.1 0.8 convolution_bitcast_fusion.5
  200.9 0.7 convolution_bitcast_fusion.3
  201.6 1.6 copy.37
  203.3 206.3 %reduce-scatter.3.cloned.1.call-done = f32[16,4,128]{2,0,1:T(8,128)} async-done(((f32[16,128,128]{2,0,1:T(8,128)}), f32[16,4,128]{2,0,1:T(8,128)}) %reduce-scatter.3.cloned.1.call-update) | async-done | bytes 32784 | tf_op jit(solution)/shard_map/reduce_scatter | solution.py:78
  409.6 0.8 slice_add_fusion.1
  411.3 20.9 %psum.38 = f32[8192]{0:T(1024)S(1)} all-reduce(f32[8192]{0:T(1024)S(1)} %get-tuple-element.9), channel_id=1, replica_groups=mesh['region'=32,'comm'=8] {'comm'}, use_global_device_ids=true, to_apply=%region_10.13 | all-reduce | flops 8192 | bytes 65536 | tf_op jit(solution)/shard_map/psum | solution.py:67
  432.2 55.1 %all-gather.5.cloned.1.call-done = f32[16,16384]{1,0:T(8,128)} async-done(((f32[16,512]{1,0:T(8,128)}), f32[16,16384]{1,0:T(8,128)}) %all-gather.5.cloned.1.call-update) | async-done | bytes 1048592 | tf_op jit(solution)/shard_map/all_gather | solution.py:52
  487.3 1.3 copy_bitcast_fusion
  489.3 0.8 gather_fusion.3
  490.1 9.6 %bitcast_reduce_fusion = f32[16,64,128]{2,0,1:T(8,128)S(1)} fusion(f32[128,128,128]{2,1,0:T(8,128)} %param.19, f32[128,16,128]{2,1,0:T(8,128)S(1)} %gather_fusion.3, pred[128]{0:T(512)(128)(4,1)S(1)} %compare_and_fusion), kind=kOutput, calls=%fused_computation.12 | convolution fusion | flops 403046400 | bytes 9961600 | tf_op jit(solution)/shard_map/kbn,bna->kba/dot_general | solution.py:58
  500.0 15.4 %convolution_bitcast_fusion = f32[16,128,128]{2,0,1:T(8,128)S(1)} fusion(f32[16,128,128]{2,0,1:T(8,128)S(1)} %bitcast.123, f32[128,128,128]{2,1,0:T(8,128)} %param.19), kind=kOutput, calls=%fused_computation.4 | convolution fusion | flops 402653184 | bytes 10485760 | tf_op jit(solution)/shard_map/kba,bna->kbn/dot_general | solution.py:72
  515.4 0.8 convolution_bitcast_fusion.4
  516.2 0.7 convolution_bitcast_fusion.2
  516.9 1.6 copy.44
  518.7 20.7 %psum.39 = f32[8192]{0:T(1024)S(1)} all-reduce(f32[8192]{0:T(1024)S(1)} %fusion.31), channel_id=1, replica_groups=mesh['region'=32,'comm'=8] {'comm'}, use_global_device_ids=true, to_apply=%region_12.15 | all-reduce | flops 8192 | bytes 65536 | tf_op jit(solution)/shard_map/psum | solution.py:67
  540.0 190.4 %reduce-scatter.5.cloned.1.call-done = f32[16,4,128]{2,0,1:T(8,128)} async-done(((f32[16,128,128]{2,0,1:T(8,128)}), f32[16,4,128]{2,0,1:T(8,128)}) %reduce-scatter.5.cloned.1.call-update) | async-done | bytes 32784 | tf_op jit(solution)/shard_map/reduce_scatter | solution.py:78
  730.3 0.8 slice_add_fusion
  731.1 0.9 fusion.25
  (52 shorter events, 4.6 us)
Async XLA Ops:
  7.2 177.0 %copy-start = (f32[16,8192]{1,0:T(8,128)S(1)}, f32[16,8192]{1,0:T(8,128)}, u32[]{:S(2)}) copy-start(f32[16,8192]{1,0:T(8,128)} %param.13) | copy-start | bytes 1572868
  7.2 177.0 %copy-start.6 = (f32[8192]{0:T(1024)S(1)}, f32[8192]{0:T(1024)}, u32[]{:S(2)}) copy-start(f32[8192]{0:T(1024)} %param.16) | copy-start | bytes 98308
  7.2 177.0 %copy-start.2 = (f32[16,8192]{1,0:T(8,128)S(1)}, f32[16,8192]{1,0:T(8,128)}, u32[]{:S(2)}) copy-start(f32[16,8192]{1,0:T(8,128)} %param.14) | copy-start | bytes 1572868
  7.2 164.6 %all-gather.3.cloned.1.call-start = ((), (), s32[]{:S(2)}) async-start(), calls=%async_computation.2 | async-start | bytes 1081344 | tf_op jit(solution)/shard_map/all_gather | solution.py:52
  8.7 400.9 %reduce-scatter.3.cloned.1.call-start = ((), (), s32[]{:S(2)}) async-start(), calls=%async_computation.3 | async-start | bytes 1081344 | tf_op jit(solution)/shard_map/reduce_scatter | solution.py:78
  184.2 15.9 %copy-start.7 = (s32[128]{0:T(128)S(1)}, s32[128]{0:T(128)}, u32[]{:S(2)}) copy-start(s32[128]{0:T(128)} %param.20) | copy-start | bytes 1540
  184.2 16.6 %copy-start.8 = (s32[8]{0:T(128)S(1)}, s32[8]{0:T(128)}, u32[]{:S(2)}) copy-start(s32[8]{0:T(128)} %param.21) | copy-start | bytes 100
  184.6 225.8 %copy-start.1 = (f32[16,4096]{1,0:T(8,128)S(1)}, f32[16,4096]{1,0:T(8,128)}, u32[]{:S(2)}) copy-start(f32[16,4096]{1,0:T(8,128)} %param.17) | copy-start | bytes 786436
  184.6 225.8 %copy-start.4 = (f32[16,4096]{1,0:T(8,128)S(1)}, f32[16,4096]{1,0:T(8,128)}, u32[]{:S(2)}) copy-start(f32[16,4096]{1,0:T(8,128)} %param.18) | copy-start | bytes 786436
  184.6 247.5 %copy-start.5 = (f32[8192]{0:T(1024)S(1)}, f32[8192]{0:T(1024)}, u32[]{:S(2)}) copy-start(f32[8192]{0:T(1024)} %param.15) | copy-start | bytes 98308
  203.2 284.1 %all-gather.5.cloned.1.call-start = ((), (), s32[]{:S(2)}) async-start(), calls=%async_computation.4 | async-start | bytes 1081344 | tf_op jit(solution)/shard_map/all_gather | solution.py:52
  411.3 319.1 %reduce-scatter.5.cloned.1.call-start = ((), (), s32[]{:S(2)}) async-start(), calls=%async_computation.5 | async-start | bytes 1081344 | tf_op jit(solution)/shard_map/reduce_scatter | solution.py:78
  499.8 18.7 %copy-start.3 = (f32[16,8192]{1,0:T(8,128)}, f32[16,8192]{1,0:T(8,128)S(1)}, u32[]{:S(2)}) copy-start(f32[16,8192]{1,0:T(8,128)S(1)} %get-tuple-element.8) | copy-start | bytes 1572868
Sparse Core Ops, SparseCore 0:
  11.2 78.9 all-gather.2
  203.3 206.2 reduce-scatter.2
  412.8 74.4 all-gather.4
  518.6 211.6 reduce-scatter.4
where the time goes:
time: 739 us
  waiting for transfers between devices  452 us (61%)
  blocking collectives  194 us (26%)
  matrix products  53 us (7%)
  between operations  16.2 us (2%)
  local copies, waits for them, and re-layouts  11.8 us (2%)
  other arithmetic  11.5 us (2%)
    reduce_scatter x2, waiting for transfers between devices, body(): lax.psum_scatter(routed, 'region', scatter_dimension=1, tiled=True)  397 us
    psum x1, blocking collectives, body(): cost_all, demand_all = lax.psum((cost_sq, demand_sq), ('region', 'comm'))  79.2 us
    psum x1, blocking collectives, body(): capacity_all = lax.psum(capacity_sq, 'region')  73.2 us
    all_gather x2, waiting for transfers between devices, body(): lax.all_gather(node_dual[:, :edge_cols], 'region', axis=1, tiled=True)  55.1 us
    psum x2, blocking collectives, body(): load_total = lax.psum(arc_load, 'comm')  41.5 us
    dot_general x2, matrix products, body(): jnp.einsum('kba,bna->kbn', repeated_flow, incidence, precision=highest)  30.9 us
    dot_general x2, matrix products, body(): jnp.einsum('kbn,bna->kba', chosen_duals, incidence, precision=highest)  19.2 us
  transfers between devices with their start and end apart: 4, of which 3 were waited for; matrix products, arithmetic and copies ran while one was open for 1% of the time, Pallas kernels for 0%

commit v1 on v0

--- a/solution.py
+++ b/solution.py
@@ -64,7 +64,7 @@
         flow_new = jnp.maximum(flow_now - primal_step * (cost - back_term + cap_dual[None, :]), 0.0)
         flow_bar = 2.0 * flow_new - flow_now
         arc_load = jnp.sum(flow_bar, axis=0)
-        load_total = lax.psum(arc_load, "comm")
+        load_total = jnp.sum(lax.all_gather(arc_load, "comm"), axis=0)
         cap_dual = jnp.maximum(cap_dual + dual_step * (load_total - capacity), 0.0)
         repeated_flow = jnp.repeat(
             flow_bar.reshape(commodities, arc_count // block_width, block_width), BPA, axis=1

time: 739 us -> 739 us (level)
  blocking collectives: 194 us -> 178 us
  waiting for transfers between devices: 452 us -> 467 us
    psum x2 -> x0, blocking collectives: 41.5 us -> none  [body(): load_total = lax.psum(arc_load, 'comm')]
    all_gather x0 -> x2, blocking collectives: none -> 25.9 us  [body(): load_total = jnp.sum(lax.all_gather(arc_load, 'comm'), axis=0)]
    all_gather x2, waiting for transfers between devices: 55.1 us -> 62.8 us  [body(): lax.all_gather(node_dual[:, :edge_cols], 'region', axis=1, tiled=True)]
    reduce_scatter x2, waiting for transfers between devices: 397 us -> 404 us  [body(): lax.psum_scatter(routed, 'region', scatter_dimension=1, tiled=True)]
where the time goes in v1:
time: 739 us
  waiting for transfers between devices  467 us (63%)
  blocking collectives  178 us (24%)
  matrix products  53 us (7%)
  between operations  16.2 us (2%)
  local copies, waits for them, and re-layouts  11.9 us (2%)
  other arithmetic  11.7 us (2%)
    reduce_scatter x2, waiting for transfers between devices, body(): lax.psum_scatter(routed, 'region', scatter_dimension=1, tiled=True)  404 us
    psum x1, blocking collectives, body(): cost_all, demand_all = lax.psum((cost_sq, demand_sq), ('region', 'comm'))  79.2 us
    psum x1, blocking collectives, body(): capacity_all = lax.psum(capacity_sq, 'region')  73.2 us
    all_gather x2, waiting for transfers between devices, body(): lax.all_gather(node_dual[:, :edge_cols], 'region', axis=1, tiled=True)  62.8 us
    dot_general x2, matrix products, body(): jnp.einsum('kba,bna->kbn', repeated_flow, incidence, precision=highest)  30.9 us
    all_gather x2, blocking collectives, body(): load_total = jnp.sum(lax.all_gather(arc_load, 'comm'), axis=0)  25.9 us
    dot_general x2, matrix products, body(): jnp.einsum('kbn,bna->kba', chosen_duals, incidence, precision=highest)  19.2 us
  transfers between devices with their start and end apart: 4, of which 3 were waited for; matrix products, arithmetic and copies ran while one was open for 1% of the time, Pallas kernels for 0%

profile of v1, /device:TPU:8, one launch (start us, length us, event | category | flops | bytes accessed | tf_op | source)
XLA Modules:
  0.0 738.6 jit_solution(11486823875616351913)
XLA Ops:
  7.2 1.5 slice.30
  8.8 1.6 multiply_reduce_fusion.1
  10.4 1.8 multiply_reduce_fusion
  12.2 1.4 multiply_reduce_fusion.2
  13.6 79.2 %all-reduce = (f32[]{:T(128)}, f32[]{:T(128)}) all-reduce(f32[]{:T(128)} %multiply_reduce_fusion, f32[]{:T(128)} %multiply_reduce_fusion.1), channel_id=1, replica_groups=mesh['region'=32,'comm'=8] {'region','comm'}, use_global_device_ids=true, to_apply=%region_1.0 | all-reduce | flops 2 | bytes 16 | tf_op jit(solution)/shard_map/psum | solution.py:38
  92.9 73.2 %psum.23 = f32[]{:T(128)} all-reduce(f32[]{:T(128)} %multiply_reduce_fusion.2), channel_id=1, replica_groups=mesh['region'=32,'comm'=8] {'region'}, use_global_device_ids=true, to_apply=%region_5.0 | all-reduce | flops 1 | bytes 8 | tf_op jit(solution)/shard_map/psum | solution.py:39
  168.2 0.7 compare_select_fusion.1
  169.5 0.7 compare_and_fusion
  170.1 0.7 compare_and_fusion.1
  170.8 1.0 copy_bitcast_fusion.5
  171.8 1.3 copy_bitcast_fusion.1
  173.8 0.8 gather_fusion.1
  174.6 9.6 %bitcast_reduce_fusion.1 = f32[16,64,128]{2,0,1:T(8,128)S(1)} fusion(f32[128,128,128]{2,1,0:T(8,128)} %param.19, f32[128,16,128]{2,1,0:T(8,128)S(1)} %gather_fusion.1, pred[128]{0:T(512)(128)(4,1)S(1)} %compare_and_fusion), kind=kOutput, calls=%fused_computation.13 | convolution fusion | flops 403046400 | bytes 9961600 | tf_op jit(solution)/shard_map/kbn,bna->kba/dot_general | solution.py:58
  184.7 15.4 %convolution_bitcast_fusion.1 = f32[16,128,128]{2,0,1:T(8,128)S(1)} fusion(f32[16,128,128]{2,0,1:T(8,128)S(1)} %bitcast.122, f32[128,128,128]{2,1,0:T(8,128)} %param.19), kind=kOutput, calls=%fused_computation.5 | convolution fusion | flops 402653184 | bytes 10485760 | tf_op jit(solution)/shard_map/kba,bna->kbn/dot_general | solution.py:72
  200.1 0.8 convolution_bitcast_fusion.5
  200.9 0.7 convolution_bitcast_fusion.3
  201.6 1.6 copy.51
  203.3 206.3 %reduce-scatter.3.cloned.1.call-done = f32[16,4,128]{2,0,1:T(8,128)} async-done(((f32[16,128,128]{2,0,1:T(8,128)}), f32[16,4,128]{2,0,1:T(8,128)}) %reduce-scatter.3.cloned.1.call-update) | async-done | bytes 32784 | tf_op jit(solution)/shard_map/reduce_scatter | solution.py:78
  409.6 0.8 slice_add_fusion.1
  411.3 13.1 %all-gather = f32[65536]{0:T(1024)S(1)} all-gather(f32[8192]{0:T(1024)S(1)} %get-tuple-element.9), channel_id=2, replica_groups=mesh['region'=32,'comm'=8] {'comm'}, dimensions={0}, use_global_device_ids=true | all-gather | bytes 294912 | tf_op jit(solution)/shard_map/all_gather | solution.py:67
  424.6 62.7 %all-gather.7.cloned.1.call-done = f32[16,16384]{1,0:T(8,128)} async-done(((f32[16,512]{1,0:T(8,128)}), f32[16,16384]{1,0:T(8,128)}) %all-gather.7.cloned.1.call-update) | async-done | bytes 1048592 | tf_op jit(solution)/shard_map/all_gather | solution.py:52
  487.3 1.3 copy_bitcast_fusion
  489.3 0.8 gather_fusion.3
  490.1 9.6 %bitcast_reduce_fusion = f32[16,64,128]{2,0,1:T(8,128)S(1)} fusion(f32[128,128,128]{2,1,0:T(8,128)} %param.19, f32[128,16,128]{2,1,0:T(8,128)S(1)} %gather_fusion.3, pred[128]{0:T(512)(128)(4,1)S(1)} %compare_and_fusion), kind=kOutput, calls=%fused_computation.12 | convolution fusion | flops 403046400 | bytes 9961600 | tf_op jit(solution)/shard_map/kbn,bna->kba/dot_general | solution.py:58
  500.0 15.4 %convolution_bitcast_fusion = f32[16,128,128]{2,0,1:T(8,128)S(1)} fusion(f32[16,128,128]{2,0,1:T(8,128)S(1)} %bitcast.123, f32[128,128,128]{2,1,0:T(8,128)} %param.19), kind=kOutput, calls=%fused_computation.4 | convolution fusion | flops 402653184 | bytes 10485760 | tf_op jit(solution)/shard_map/kba,bna->kbn/dot_general | solution.py:72
  515.4 0.8 convolution_bitcast_fusion.4
  516.2 0.7 convolution_bitcast_fusion.2
  516.9 1.6 copy.58
  518.7 12.9 %all-gather.1 = f32[65536]{0:T(1024)S(1)} all-gather(f32[8192]{0:T(1024)S(1)} %fusion.31), channel_id=3, replica_groups=mesh['region'=32,'comm'=8] {'comm'}, dimensions={0}, use_global_device_ids=true | all-gather | bytes 294912 | tf_op jit(solution)/shard_map/all_gather | solution.py:67
  532.3 198.0 %reduce-scatter.5.cloned.1.call-done = f32[16,4,128]{2,0,1:T(8,128)} async-done(((f32[16,128,128]{2,0,1:T(8,128)}), f32[16,4,128]{2,0,1:T(8,128)}) %reduce-scatter.5.cloned.1.call-update) | async-done | bytes 32784 | tf_op jit(solution)/shard_map/reduce_scatter | solution.py:78
  730.3 0.8 slice_add_fusion
  731.1 0.9 fusion.25
  (56 shorter events, 4.8 us)
Async XLA Ops:
  7.2 177.0 %copy-start = (f32[16,8192]{1,0:T(8,128)S(1)}, f32[16,8192]{1,0:T(8,128)}, u32[]{:S(2)}) copy-start(f32[16,8192]{1,0:T(8,128)} %param.13) | copy-start | bytes 1572868
  7.2 177.0 %copy-start.6 = (f32[8192]{0:T(1024)S(1)}, f32[8192]{0:T(1024)}, u32[]{:S(2)}) copy-start(f32[8192]{0:T(1024)} %param.16) | copy-start | bytes 98308
  7.2 177.0 %copy-start.2 = (f32[16,8192]{1,0:T(8,128)S(1)}, f32[16,8192]{1,0:T(8,128)}, u32[]{:S(2)}) copy-start(f32[16,8192]{1,0:T(8,128)} %param.14) | copy-start | bytes 1572868
  7.2 164.6 %all-gather.5.cloned.1.call-start = ((), (), s32[]{:S(2)}) async-start(), calls=%async_computation.2 | async-start | bytes 1081344 | tf_op jit(solution)/shard_map/all_gather | solution.py:52
  8.7 400.9 %reduce-scatter.3.cloned.1.call-start = ((), (), s32[]{:S(2)}) async-start(), calls=%async_computation.3 | async-start | bytes 1081344 | tf_op jit(solution)/shard_map/reduce_scatter | solution.py:78
  184.2 15.9 %copy-start.7 = (s32[128]{0:T(128)S(1)}, s32[128]{0:T(128)}, u32[]{:S(2)}) copy-start(s32[128]{0:T(128)} %param.20) | copy-start | bytes 1540
  184.2 16.6 %copy-start.8 = (s32[8]{0:T(128)S(1)}, s32[8]{0:T(128)}, u32[]{:S(2)}) copy-start(s32[8]{0:T(128)} %param.21) | copy-start | bytes 100
  184.6 225.8 %copy-start.1 = (f32[16,4096]{1,0:T(8,128)S(1)}, f32[16,4096]{1,0:T(8,128)}, u32[]{:S(2)}) copy-start(f32[16,4096]{1,0:T(8,128)} %param.17) | copy-start | bytes 786436
  184.6 225.8 %copy-start.4 = (f32[16,4096]{1,0:T(8,128)S(1)}, f32[16,4096]{1,0:T(8,128)}, u32[]{:S(2)}) copy-start(f32[16,4096]{1,0:T(8,128)} %param.18) | copy-start | bytes 786436
  184.6 239.9 %copy-start.5 = (f32[8192]{0:T(1024)S(1)}, f32[8192]{0:T(1024)}, u32[]{:S(2)}) copy-start(f32[8192]{0:T(1024)} %param.15) | copy-start | bytes 98308
  203.2 284.1 %all-gather.7.cloned.1.call-start = ((), (), s32[]{:S(2)}) async-start(), calls=%async_computation.4 | async-start | bytes 1081344 | tf_op jit(solution)/shard_map/all_gather | solution.py:52
  411.3 319.1 %reduce-scatter.5.cloned.1.call-start = ((), (), s32[]{:S(2)}) async-start(), calls=%async_computation.5 | async-start | bytes 1081344 | tf_op jit(solution)/shard_map/reduce_scatter | solution.py:78
  499.8 18.7 %copy-start.3 = (f32[16,8192]{1,0:T(8,128)}, f32[16,8192]{1,0:T(8,128)S(1)}, u32[]{:S(2)}) copy-start(f32[16,8192]{1,0:T(8,128)S(1)} %get-tuple-element.8) | copy-start | bytes 1572868
Sparse Core Ops, SparseCore 0:
  11.2 78.9 all-gather.4
  203.3 206.2 reduce-scatter.2
  412.8 74.4 all-gather.6
  518.6 211.6 reduce-scatter.4
